TPU v7x, 32 devices: a whole 2x2x4 slice. The times are simulated.
32 devices in a mesh: groups: 2 (over y), ctx: 4 (over z), heads: 2 (over x), rep: 2 (over core).
Axes of the slice: x: 2, y: 2, z: 4, core: 2. Of those that a mesh axis runs over, the one named last changes fastest.
Arguments:
- queries: bfloat16 [24576, 32, 128], P(('groups', 'ctx'), ('heads', 'rep')), parts along dimension 0, may hold values from -14 to 14
- keys: bfloat16 [24576, 8, 128], P(('groups', 'ctx'), 'heads'), parts along dimension 0, may hold values from -14 to 14
- values: bfloat16 [24576, 8, 128], P(('groups', 'ctx'), 'heads'), parts along dimension 0, may hold values from -6 to 6
- chosen: int32 [8, 192, 8], P('heads', ('groups', 'ctx')), parts along dimension 1, may hold values from 0 to 95, as said below
Outputs:
- attended: bfloat16 [24576, 32, 128], P(('groups', 'ctx'), ('heads', 'rep')), parts along dimension 0
There are 2 independent parts, one for each index of `groups`. A program takes and returns all parts, laid end to end along the dimension named above; each array names one. Nothing has to cross between parts.
Inputs may be any that keep to these rules, and one draw needn't show every extreme that they name: chosen[h, b, 0] = b. The other entries of a list are at most b and differ from each other, except that b itself may be repeated. For one key-value head, the 24 query blocks of one sequence shard list at most 2 distinct blocks of any other shard.
All inputs are finite; a program needn't handle non-finite values.
Results may differ from a plain program's by a relative error of at most 0.0046.
Values may be sent and summed in bfloat16 or wider, within the bound.
A program may use at most 128 MiB of HBM per device.

v0:
```python
import jax
import jax.numpy as jnp
from jax import lax
from jax.sharding import PartitionSpec as P

QUERY_HEADS = 32
KEY_VALUE_HEADS = 8
REMOTE_BLOCK_MAX = 2


def attend(query_part, key_part, value_part, chosen_part):
    block_len = query_part.shape[1]
    head_dim = query_part.shape[-1]
    picks = chosen_part.shape[-1]
    scores = jnp.einsum(
        "gqeah,egkh->egaqk", query_part, key_part, preferred_element_type=jnp.float32
    ) * head_dim ** (-0.5)
    earlier = chosen_part[..., :, None] == chosen_part[..., None, :]
    before_slot = jnp.arange(picks)[:, None] > jnp.arange(picks)[None, :]
    repeated = jnp.any(earlier & before_slot[None, None], axis=-1)
    slot_open = jnp.repeat(jnp.logical_not(repeated), block_len, axis=-1)
    key_slot = jnp.arange(picks * block_len) // block_len
    key_place = jnp.arange(picks * block_len) % block_len
    query_place = jnp.arange(block_len)
    causal = (key_slot[None, :] > 0) | (key_place[None, :] <= query_place[:, None])
    visible = slot_open[:, :, None, None, :] & causal[None, None, None]
    highest = jnp.max(jnp.where(visible, scores, -jnp.inf), axis=-1, keepdims=True)
    weights = jnp.where(visible, jnp.exp(scores - highest), jnp.float32(0.0))
    totals = jnp.sum(weights, axis=-1)
    probabilities = weights.astype(jnp.bfloat16)
    attended = jnp.einsum(
        "egaqk,egkh->gqeah", probabilities, value_part, preferred_element_type=jnp.float32
    )
    scaled = attended / jnp.transpose(totals, (1, 3, 0, 2))[..., None]
    return scaled.astype(jnp.bfloat16)


def on_device(queries, keys, values, chosen):
    tokens_dev, query_heads, head_dim = queries.shape
    blocks = chosen.shape[1]
    picks = chosen.shape[2]
    block_len = tokens_dev // blocks
    heads_per_group = QUERY_HEADS // KEY_VALUE_HEADS
    used_heads = max(1, query_heads // heads_per_group)
    per_head = query_heads // used_heads
    shard_count = lax.axis_size("ctx")
    position = lax.axis_index("ctx")
    rep_index = lax.axis_index("rep")
    first_head = rep_index * query_heads // heads_per_group
    chosen_used = lax.dynamic_slice_in_dim(chosen, first_head, used_heads, 0)
    fetch_keys = lax.dynamic_slice_in_dim(keys, first_head, used_heads, 1)
    fetch_values = lax.dynamic_slice_in_dim(values, first_head, used_heads, 1)
    fetch_heads = chosen_used.shape[0]
    flat_chosen = chosen_used.reshape(fetch_heads, blocks * picks)
    needed = jnp.any(
        flat_chosen[:, :, None] == jnp.arange(shard_count * blocks, dtype=jnp.int32)[None, None, :],
        axis=1,
    )
    needed = (
        needed.reshape(fetch_heads, shard_count, blocks)
        & (jnp.arange(shard_count, dtype=jnp.int32) != position)[None, :, None]
    )
    ranking = jnp.cumsum(needed.astype(jnp.int32), axis=2) - 1
    matches = needed[..., None] & (
        ranking[..., None] == jnp.arange(REMOTE_BLOCK_MAX, dtype=jnp.int32)[None, None, None, :]
    )
    request = jnp.sum(
        matches.astype(jnp.int32) * jnp.arange(blocks, dtype=jnp.int32)[None, None, :, None], axis=2
    )
    requests_in = lax.all_to_all(request, "ctx", split_axis=1, concat_axis=1, tiled=True)
    key_blocks = jnp.transpose(fetch_keys, (1, 0, 2)).reshape(
        fetch_heads, blocks, block_len, head_dim
    )
    value_blocks = jnp.transpose(fetch_values, (1, 0, 2)).reshape(
        fetch_heads, blocks, block_len, head_dim
    )
    fetch_index = jnp.arange(fetch_heads, dtype=jnp.int32)[:, None, None]
    send_keys = key_blocks[fetch_index, requests_in].reshape(
        fetch_heads, shard_count, REMOTE_BLOCK_MAX * block_len, head_dim
    )
    send_values = value_blocks[fetch_index, requests_in].reshape(
        fetch_heads, shard_count, REMOTE_BLOCK_MAX * block_len, head_dim
    )
    got_keys, got_values = (
        lax.all_to_all(send_keys, "ctx", split_axis=1, concat_axis=1, tiled=True),
        lax.all_to_all(send_values, "ctx", split_axis=1, concat_axis=1, tiled=True),
    )
    remote_keys = got_keys.reshape(used_heads, shard_count * REMOTE_BLOCK_MAX, block_len, head_dim)
    remote_values = got_values.reshape(
        used_heads, shard_count * REMOTE_BLOCK_MAX, block_len, head_dim
    )
    rank_used = ranking.reshape(used_heads, shard_count * blocks)
    key_table = jnp.concatenate([key_blocks, remote_keys], axis=1)
    value_table = jnp.concatenate([value_blocks, remote_values], axis=1)
    source = chosen_used // blocks
    within = chosen_used % blocks
    slot_rank = jnp.take_along_axis(
        rank_used, chosen_used.reshape(used_heads, blocks * picks), axis=1
    ).reshape(used_heads, blocks, picks)
    slot_index = jnp.where(
        source == position, within, blocks + source * REMOTE_BLOCK_MAX + slot_rank
    )
    group_size = 4
    query_groups = queries.reshape(
        blocks // group_size, group_size, block_len, used_heads, per_head, head_dim
    )
    index_groups = jnp.transpose(
        slot_index.reshape(used_heads, blocks // group_size, group_size, picks), (1, 0, 2, 3)
    )
    chosen_groups = jnp.transpose(
        chosen_used.reshape(used_heads, blocks // group_size, group_size, picks), (1, 0, 2, 3)
    )
    head_index = jnp.arange(used_heads, dtype=jnp.int32)[:, None, None]

    def block_group(operands):
        query_part, index_part, chosen_part = operands
        key_part = key_table[head_index, index_part].reshape(
            used_heads, group_size, picks * block_len, head_dim
        )
        value_part = value_table[head_index, index_part].reshape(
            used_heads, group_size, picks * block_len, head_dim
        )
        return attend(query_part, key_part, value_part, chosen_part)

    result = lax.map(block_group, (query_groups, index_groups, chosen_groups))
    return result.reshape(tokens_dev, query_heads, head_dim)


def solution(mesh):
    placed = (
        P(("groups", "ctx"), ("heads", "rep"), None),
        P(("groups", "ctx"), "heads", None),
        P(("groups", "ctx"), "heads", None),
        P("heads", ("groups", "ctx"), None),
    )
    return jax.shard_map(
        on_device,
        mesh=mesh,
        in_specs=placed,
        out_specs=P(("groups", "ctx"), ("heads", "rep"), None),
        check_vma=False,
    )
```

profile of v0, /device:TPU:0, one launch (start us, length us, event | category | flops | bytes accessed | tf_op | source)
XLA Modules:
  0.0 322.3 jit_solution(5121647006889984484)
XLA Ops:
  2.5 6.3 %all-to-all-start = ((s32[2,4,2]{2,0,1:T(2,128)}), s32[2,4,2]{2,0,1:T(2,128)S(1)}, u32[]{:S(2)}, u32[]{:S(2)}) async-start(s32[2,4,2]{2,0,1:T(2,128)} %copy.57), calls=%async_computation | async-start | bytes 8192 | tf_op jit(solution)/shard_map/all_to_all | solution.py:70
  8.8 6.2 %dynamic-slice_bitcast_fusion.1 = (bf16[2,3072,128]{2,0,1:T(2,128)(2,1)}, bf16[2,3072,128]{2,0,1:T(2,128)(2,1)S(1)}) fusion(bf16[3072,4,128]{2,1,0:T(4,128)(2,1)} %param.7, s32[]{:T(128)S(6)} %select_n.118, bf16[3072,4,128]{2,1,0:T(4,128)(2,1)} %param.8), kind=kLoop, calls=%fused_computation.54 | loop fusion | bytes 6291460 | tf_op jit(solution)/shard_map/transpose | solution.py:71
  17.1 5.1 %all-to-all-start.1 = ((bf16[2,4,256,128]{3,2,0,1:T(8,128)(2,1)}), bf16[2,4,256,128]{3,2,0,1:T(8,128)(2,1)}, u32[]{:S(2)}, u32[]{:S(2)}) async-start(bf16[2,4,256,128]{3,2,0,1:T(8,128)(2,1)} %copy.60), calls=%async_computation.1 | async-start | bytes 1048576 | tf_op jit(solution)/shard_map/all_to_all | solution.py:86
  27.1 9.1 %all-to-all-done.1 = bf16[2,4,256,128]{3,2,0,1:T(8,128)(2,1)} async-done(((bf16[2,4,256,128]{3,2,0,1:T(8,128)(2,1)}), bf16[2,4,256,128]{3,2,0,1:T(8,128)(2,1)}, u32[]{:S(2)}, u32[]{:S(2)}) %all-to-all-start.1) | async-done | bytes 524320 | tf_op jit(solution)/shard_map/all_to_all | solution.py:86
  36.2 4.3 %all-to-all-start.2 = ((bf16[2,4,256,128]{3,2,0,1:T(8,128)(2,1)}), bf16[2,4,256,128]{3,2,0,1:T(8,128)(2,1)}, u32[]{:S(2)}, u32[]{:S(2)}) async-start(bf16[2,4,256,128]{3,2,0,1:T(8,128)(2,1)} %copy.63), calls=%async_computation.2 | async-start | bytes 1048576 | tf_op jit(solution)/shard_map/all_to_all | solution.py:85
  40.8 3.5 %gather_fusion.4 = s32[384]{0:T(512)S(1)} fusion(s32[2,96]{1,0:T(2,128)S(1)} %sub.39, s32[384]{0:T(512)S(1)} %reshape.284), kind=kCustom, calls=%fused_computation.4 | custom fusion | bytes 6144 | tf_op jit(solution)/shard_map/jit(take_along_axis)/gather | solution.py:97
  47.2 7.3 %all-to-all-done.2 = bf16[2,4,256,128]{3,2,0,1:T(8,128)(2,1)} async-done(((bf16[2,4,256,128]{3,2,0,1:T(8,128)(2,1)}), bf16[2,4,256,128]{3,2,0,1:T(8,128)(2,1)}, u32[]{:S(2)}, u32[]{:S(2)}) %all-to-all-start.2) | async-done | bytes 524320 | tf_op jit(solution)/shard_map/all_to_all | solution.py:85
  57.0 264.6 %while.13 = (s32[]{:T(128)}, bf16[6,4,128,2,4,128]{5,4,3,2,1,0:T(4,128)(2,1)}, s32[6,2,4,8]{3,2,0,1:T(4,128)S(1)}, bf16[2,32,128,128]{3,2,1,0:T(8,128)(2,1)}, s3...) while((s32[]{:T(128)}, ...), condition=%wide.region_7.8_spmd.clone, body=%wide.region_3.7_spmd.clone.sunk | while | flops 2179221504 | bytes 82130696 | solution.py:125
  57.2 2.6 gather_fusion
  61.3 8.1 %fusion.69 = f32[2,4,1024,128,4]{3,2,4,1,0:T(8,128)} fusion(bf16[2,4,1024,128,1]{3,2,4,1,0:T(8,128)(2,1)S(1)} %bitcast.94, bf16[1,4,128,2,4,128]{5,4,3,2,1,0:T(4,128)(2,1)S(1)} %constant_dynamic-slice_fusion.3), kind=kOutput, calls=%fused_computation.23.clone.1 | convolution fusion | flops 1073741824 | bytes 19922944 | tf_op jit(solution)/shard_map/while/body/eval_jaxpr/gqeah,egkh->egaqk/dot_general | solution.py:15
  71.6 19.8 %fusion.73 = (bf16[2,4,4,128,1024]{3,4,2,1,0:T(8,128)(2,1)}, f32[2,4,4,128]{3,2,1,0:T(4,128)S(1)}) fusion(f32[2,4,1024,128,4]{3,2,4,1,0:T(8,128)} %fusion.69, pred[2,4,128,1024]{2,3,1,0:T(8,128)(4,1)S(1)} %broadcast_and_fusion.4), kind=kOutput, calls=%fused_computation.81.clone.1 | output fusion | flops 29361152 | bytes 26230784 | tf_op jit(solution)/shard_map/while/body/eval_jaxpr/sub | solution.py:28
  93.6 5.4 %fusion.74 = bf16[1,4,128,2,4,128]{2,5,4,3,1,0:T(8,128)(2,1)S(1)} fusion(bf16[2,4,4,128,1024]{3,4,2,1,0:T(8,128)(2,1)} %get-tuple-element.220, bf16[2,4,1024,128,1]{3,2,1,0,4:T(8,128)(2,1)} %bitcast.95, f32[2,4,4,128]{3,2,1,0:T(4,128)S(1)} %get-tuple-element.221), kind=kOutput, calls=%fused_computation.24.clone.1 | convolution fusion | flops 1074790400 | bytes 11550720 | tf_op jit(solution)/shard_map/while/body/eval_jaxpr/egaqk,egkh->gqeah/dot_general | solution.py:31
  101.3 2.6 gather_fusion
  105.4 8.1 %fusion.69 = f32[2,4,1024,128,4]{3,2,4,1,0:T(8,128)} fusion(bf16[2,4,1024,128,1]{3,2,4,1,0:T(8,128)(2,1)S(1)} %bitcast.94, bf16[1,4,128,2,4,128]{5,4,3,2,1,0:T(4,128)(2,1)S(1)} %constant_dynamic-slice_fusion.3), kind=kOutput, calls=%fused_computation.23.clone.1 | convolution fusion | flops 1073741824 | bytes 19922944 | tf_op jit(solution)/shard_map/while/body/eval_jaxpr/gqeah,egkh->egaqk/dot_general | solution.py:15
  115.7 19.8 %fusion.73 = (bf16[2,4,4,128,1024]{3,4,2,1,0:T(8,128)(2,1)}, f32[2,4,4,128]{3,2,1,0:T(4,128)S(1)}) fusion(f32[2,4,1024,128,4]{3,2,4,1,0:T(8,128)} %fusion.69, pred[2,4,128,1024]{2,3,1,0:T(8,128)(4,1)S(1)} %broadcast_and_fusion.4), kind=kOutput, calls=%fused_computation.81.clone.1 | output fusion | flops 29361152 | bytes 26230784 | tf_op jit(solution)/shard_map/while/body/eval_jaxpr/sub | solution.py:28
  137.7 5.4 %fusion.74 = bf16[1,4,128,2,4,128]{2,5,4,3,1,0:T(8,128)(2,1)S(1)} fusion(bf16[2,4,4,128,1024]{3,4,2,1,0:T(8,128)(2,1)} %get-tuple-element.220, bf16[2,4,1024,128,1]{3,2,1,0,4:T(8,128)(2,1)} %bitcast.95, f32[2,4,4,128]{3,2,1,0:T(4,128)S(1)} %get-tuple-element.221), kind=kOutput, calls=%fused_computation.24.clone.1 | convolution fusion | flops 1074790400 | bytes 11550720 | tf_op jit(solution)/shard_map/while/body/eval_jaxpr/egaqk,egkh->gqeah/dot_general | solution.py:31
  145.4 2.6 gather_fusion
  149.5 8.1 %fusion.69 = f32[2,4,1024,128,4]{3,2,4,1,0:T(8,128)} fusion(bf16[2,4,1024,128,1]{3,2,4,1,0:T(8,128)(2,1)S(1)} %bitcast.94, bf16[1,4,128,2,4,128]{5,4,3,2,1,0:T(4,128)(2,1)S(1)} %constant_dynamic-slice_fusion.3), kind=kOutput, calls=%fused_computation.23.clone.1 | convolution fusion | flops 1073741824 | bytes 19922944 | tf_op jit(solution)/shard_map/while/body/eval_jaxpr/gqeah,egkh->egaqk/dot_general | solution.py:15
  159.8 19.8 %fusion.73 = (bf16[2,4,4,128,1024]{3,4,2,1,0:T(8,128)(2,1)}, f32[2,4,4,128]{3,2,1,0:T(4,128)S(1)}) fusion(f32[2,4,1024,128,4]{3,2,4,1,0:T(8,128)} %fusion.69, pred[2,4,128,1024]{2,3,1,0:T(8,128)(4,1)S(1)} %broadcast_and_fusion.4), kind=kOutput, calls=%fused_computation.81.clone.1 | output fusion | flops 29361152 | bytes 26230784 | tf_op jit(solution)/shard_map/while/body/eval_jaxpr/sub | solution.py:28
  181.8 5.4 %fusion.74 = bf16[1,4,128,2,4,128]{2,5,4,3,1,0:T(8,128)(2,1)S(1)} fusion(bf16[2,4,4,128,1024]{3,4,2,1,0:T(8,128)(2,1)} %get-tuple-element.220, bf16[2,4,1024,128,1]{3,2,1,0,4:T(8,128)(2,1)} %bitcast.95, f32[2,4,4,128]{3,2,1,0:T(4,128)S(1)} %get-tuple-element.221), kind=kOutput, calls=%fused_computation.24.clone.1 | convolution fusion | flops 1074790400 | bytes 11550720 | tf_op jit(solution)/shard_map/while/body/eval_jaxpr/egaqk,egkh->gqeah/dot_general | solution.py:31
  189.5 2.6 gather_fusion
  193.6 8.1 %fusion.69 = f32[2,4,1024,128,4]{3,2,4,1,0:T(8,128)} fusion(bf16[2,4,1024,128,1]{3,2,4,1,0:T(8,128)(2,1)S(1)} %bitcast.94, bf16[1,4,128,2,4,128]{5,4,3,2,1,0:T(4,128)(2,1)S(1)} %constant_dynamic-slice_fusion.3), kind=kOutput, calls=%fused_computation.23.clone.1 | convolution fusion | flops 1073741824 | bytes 19922944 | tf_op jit(solution)/shard_map/while/body/eval_jaxpr/gqeah,egkh->egaqk/dot_general | solution.py:15
  203.9 19.8 %fusion.73 = (bf16[2,4,4,128,1024]{3,4,2,1,0:T(8,128)(2,1)}, f32[2,4,4,128]{3,2,1,0:T(4,128)S(1)}) fusion(f32[2,4,1024,128,4]{3,2,4,1,0:T(8,128)} %fusion.69, pred[2,4,128,1024]{2,3,1,0:T(8,128)(4,1)S(1)} %broadcast_and_fusion.4), kind=kOutput, calls=%fused_computation.81.clone.1 | output fusion | flops 29361152 | bytes 26230784 | tf_op jit(solution)/shard_map/while/body/eval_jaxpr/sub | solution.py:28
  225.9 5.4 %fusion.74 = bf16[1,4,128,2,4,128]{2,5,4,3,1,0:T(8,128)(2,1)S(1)} fusion(bf16[2,4,4,128,1024]{3,4,2,1,0:T(8,128)(2,1)} %get-tuple-element.220, bf16[2,4,1024,128,1]{3,2,1,0,4:T(8,128)(2,1)} %bitcast.95, f32[2,4,4,128]{3,2,1,0:T(4,128)S(1)} %get-tuple-element.221), kind=kOutput, calls=%fused_computation.24.clone.1 | convolution fusion | flops 1074790400 | bytes 11550720 | tf_op jit(solution)/shard_map/while/body/eval_jaxpr/egaqk,egkh->gqeah/dot_general | solution.py:31
  233.6 2.6 gather_fusion
  237.8 8.1 %fusion.69 = f32[2,4,1024,128,4]{3,2,4,1,0:T(8,128)} fusion(bf16[2,4,1024,128,1]{3,2,4,1,0:T(8,128)(2,1)S(1)} %bitcast.94, bf16[1,4,128,2,4,128]{5,4,3,2,1,0:T(4,128)(2,1)S(1)} %constant_dynamic-slice_fusion.3), kind=kOutput, calls=%fused_computation.23.clone.1 | convolution fusion | flops 1073741824 | bytes 19922944 | tf_op jit(solution)/shard_map/while/body/eval_jaxpr/gqeah,egkh->egaqk/dot_general | solution.py:15
  248.0 19.8 %fusion.73 = (bf16[2,4,4,128,1024]{3,4,2,1,0:T(8,128)(2,1)}, f32[2,4,4,128]{3,2,1,0:T(4,128)S(1)}) fusion(f32[2,4,1024,128,4]{3,2,4,1,0:T(8,128)} %fusion.69, pred[2,4,128,1024]{2,3,1,0:T(8,128)(4,1)S(1)} %broadcast_and_fusion.4), kind=kOutput, calls=%fused_computation.81.clone.1 | output fusion | flops 29361152 | bytes 26230784 | tf_op jit(solution)/shard_map/while/body/eval_jaxpr/sub | solution.py:28
  270.0 5.4 %fusion.74 = bf16[1,4,128,2,4,128]{2,5,4,3,1,0:T(8,128)(2,1)S(1)} fusion(bf16[2,4,4,128,1024]{3,4,2,1,0:T(8,128)(2,1)} %get-tuple-element.220, bf16[2,4,1024,128,1]{3,2,1,0,4:T(8,128)(2,1)} %bitcast.95, f32[2,4,4,128]{3,2,1,0:T(4,128)S(1)} %get-tuple-element.221), kind=kOutput, calls=%fused_computation.24.clone.1 | convolution fusion | flops 1074790400 | bytes 11550720 | tf_op jit(solution)/shard_map/while/body/eval_jaxpr/egaqk,egkh->gqeah/dot_general | solution.py:31
  277.7 2.6 gather_fusion
  281.9 8.1 %fusion.69 = f32[2,4,1024,128,4]{3,2,4,1,0:T(8,128)} fusion(bf16[2,4,1024,128,1]{3,2,4,1,0:T(8,128)(2,1)S(1)} %bitcast.94, bf16[1,4,128,2,4,128]{5,4,3,2,1,0:T(4,128)(2,1)S(1)} %constant_dynamic-slice_fusion.3), kind=kOutput, calls=%fused_computation.23.clone.1 | convolution fusion | flops 1073741824 | bytes 19922944 | tf_op jit(solution)/shard_map/while/body/eval_jaxpr/gqeah,egkh->egaqk/dot_general | solution.py:15
  292.1 19.8 %fusion.73 = (bf16[2,4,4,128,1024]{3,4,2,1,0:T(8,128)(2,1)}, f32[2,4,4,128]{3,2,1,0:T(4,128)S(1)}) fusion(f32[2,4,1024,128,4]{3,2,4,1,0:T(8,128)} %fusion.69, pred[2,4,128,1024]{2,3,1,0:T(8,128)(4,1)S(1)} %broadcast_and_fusion.4), kind=kOutput, calls=%fused_computation.81.clone.1 | output fusion | flops 29361152 | bytes 26230784 | tf_op jit(solution)/shard_map/while/body/eval_jaxpr/sub | solution.py:28
  314.1 5.4 %fusion.74 = bf16[1,4,128,2,4,128]{2,5,4,3,1,0:T(8,128)(2,1)S(1)} fusion(bf16[2,4,4,128,1024]{3,4,2,1,0:T(8,128)(2,1)} %get-tuple-element.220, bf16[2,4,1024,128,1]{3,2,1,0,4:T(8,128)(2,1)} %bitcast.95, f32[2,4,4,128]{3,2,1,0:T(4,128)S(1)} %get-tuple-element.221), kind=kOutput, calls=%fused_computation.24.clone.1 | convolution fusion | flops 1074790400 | bytes 11550720 | tf_op jit(solution)/shard_map/while/body/eval_jaxpr/egaqk,egkh->gqeah/dot_general | solution.py:31
  (152 shorter events, 64.5 us)
Async XLA Ops:
  0.0 0.7 copy-start
  2.5 12.8 %all-to-all-start = ((s32[2,4,2]{2,0,1:T(2,128)}), s32[2,4,2]{2,0,1:T(2,128)S(1)}, u32[]{:S(2)}, u32[]{:S(2)}) async-start(s32[2,4,2]{2,0,1:T(2,128)} %copy.57), calls=%async_computation | async-start | bytes 8192 | tf_op jit(solution)/shard_map/all_to_all | solution.py:70
  17.1 19.1 %all-to-all-start.1 = ((bf16[2,4,256,128]{3,2,0,1:T(8,128)(2,1)}), bf16[2,4,256,128]{3,2,0,1:T(8,128)(2,1)}, u32[]{:S(2)}, u32[]{:S(2)}) async-start(bf16[2,4,256,128]{3,2,0,1:T(8,128)(2,1)} %copy.60), calls=%async_computation.1 | async-start | bytes 1048576 | tf_op jit(solution)/shard_map/all_to_all | solution.py:86
  36.2 18.3 %all-to-all-start.2 = ((bf16[2,4,256,128]{3,2,0,1:T(8,128)(2,1)}), bf16[2,4,256,128]{3,2,0,1:T(8,128)(2,1)}, u32[]{:S(2)}, u32[]{:S(2)}) async-start(bf16[2,4,256,128]{3,2,0,1:T(8,128)(2,1)} %copy.63), calls=%async_computation.2 | async-start | bytes 1048576 | tf_op jit(solution)/shard_map/all_to_all | solution.py:85
  71.6 19.9 %copy-start.2 = (bf16[2,32,128,128]{3,2,1,0:T(8,128)(2,1)S(1)}, bf16[2,32,128,128]{3,2,1,0:T(8,128)(2,1)}, u32[]{:S(2)}) copy-start(bf16[2,32,128,128]{3,2,1,0:T(8,128)(2,1)} %get-tuple-element.241) | copy-start | bytes 6291460 | tf_op jit(solution)/shard_map/while
  115.7 19.9 %copy-start.2 = (bf16[2,32,128,128]{3,2,1,0:T(8,128)(2,1)S(1)}, bf16[2,32,128,128]{3,2,1,0:T(8,128)(2,1)}, u32[]{:S(2)}) copy-start(bf16[2,32,128,128]{3,2,1,0:T(8,128)(2,1)} %get-tuple-element.241) | copy-start | bytes 6291460 | tf_op jit(solution)/shard_map/while
  159.8 19.9 %copy-start.2 = (bf16[2,32,128,128]{3,2,1,0:T(8,128)(2,1)S(1)}, bf16[2,32,128,128]{3,2,1,0:T(8,128)(2,1)}, u32[]{:S(2)}) copy-start(bf16[2,32,128,128]{3,2,1,0:T(8,128)(2,1)} %get-tuple-element.241) | copy-start | bytes 6291460 | tf_op jit(solution)/shard_map/while
  203.9 19.9 %copy-start.2 = (bf16[2,32,128,128]{3,2,1,0:T(8,128)(2,1)S(1)}, bf16[2,32,128,128]{3,2,1,0:T(8,128)(2,1)}, u32[]{:S(2)}) copy-start(bf16[2,32,128,128]{3,2,1,0:T(8,128)(2,1)} %get-tuple-element.241) | copy-start | bytes 6291460 | tf_op jit(solution)/shard_map/while
  248.0 19.9 %copy-start.2 = (bf16[2,32,128,128]{3,2,1,0:T(8,128)(2,1)S(1)}, bf16[2,32,128,128]{3,2,1,0:T(8,128)(2,1)}, u32[]{:S(2)}) copy-start(bf16[2,32,128,128]{3,2,1,0:T(8,128)(2,1)} %get-tuple-element.241) | copy-start | bytes 6291460 | tf_op jit(solution)/shard_map/while
  292.1 19.9 %copy-start.2 = (bf16[2,32,128,128]{3,2,1,0:T(8,128)(2,1)S(1)}, bf16[2,32,128,128]{3,2,1,0:T(8,128)(2,1)}, u32[]{:S(2)}) copy-start(bf16[2,32,128,128]{3,2,1,0:T(8,128)(2,1)} %get-tuple-element.241) | copy-start | bytes 6291460 | tf_op jit(solution)/shard_map/while
  321.6 0.7 copy-start.1
where the time goes:
time: 323 us; the launch traced here: 322 us
  other arithmetic  136 us (42%)
  matrix products  81 us (25%)
  local copies, waits for them, and re-layouts  72.9 us (23%)
  waiting for transfers between devices  16.5 us (5%)
  starting transfers between devices  15.8 us (5%)
    sub x6, other arithmetic, attend(): weights = jnp.where(visible, jnp.exp(scores - highest), jnp.float32(0.0))  119 us
    dot_general x6, matrix products, attend(): jnp.einsum('gqeah,egkh->egaqk', query_part, key_part, preferred_element_t...  48.4 us
    dot_general x6, matrix products, attend(): jnp.einsum('egaqk,egkh->gqeah', probabilities, value_part, preferred_elem...  32.6 us
    gather x6, local copies, waits for them, and re-layouts, block_group(): key_table[head_index, index_part]  15.3 us
    gather x6, local copies, waits for them, and re-layouts, block_group(): value_table[head_index, index_part]  13 us
    dynamic_update_slice x12, local copies, waits for them, and re-layouts, on_device(): result = lax.map(block_group, (query_groups, index_groups, chosen_groups))  12.3 us
    dynamic_slice x6, local copies, waits for them, and re-layouts, on_device(): result = lax.map(block_group, (query_groups, index_groups, chosen_groups))  9.55 us
    all_to_all x1, waiting for transfers between devices, on_device(): lax.all_to_all(send_values, 'ctx', split_axis=1, concat_axis=1, tiled=True)  9.14 us
  transfers between devices with their start and end apart: 3, of which 2 were waited for; matrix products, arithmetic and copies ran while one was open for 6% of the time, Pallas kernels for 0%

commit v1 on v0

--- a/solution.py
+++ b/solution.py
@@ -1,6 +1,10 @@
+import math
+
 import jax
 import jax.numpy as jnp
 from jax import lax
+from jax.experimental import pallas as pl
+from jax.experimental.pallas import tpu as pltpu
 from jax.sharding import PartitionSpec as P
 
 QUERY_HEADS = 32
@@ -8,31 +12,106 @@
 REMOTE_BLOCK_MAX = 2
 
 
-def attend(query_part, key_part, value_part, chosen_part):
-    block_len = query_part.shape[1]
-    head_dim = query_part.shape[-1]
-    picks = chosen_part.shape[-1]
-    scores = jnp.einsum(
-        "gqeah,egkh->egaqk", query_part, key_part, preferred_element_type=jnp.float32
-    ) * head_dim ** (-0.5)
-    earlier = chosen_part[..., :, None] == chosen_part[..., None, :]
-    before_slot = jnp.arange(picks)[:, None] > jnp.arange(picks)[None, :]
-    repeated = jnp.any(earlier & before_slot[None, None], axis=-1)
-    slot_open = jnp.repeat(jnp.logical_not(repeated), block_len, axis=-1)
-    key_slot = jnp.arange(picks * block_len) // block_len
-    key_place = jnp.arange(picks * block_len) % block_len
-    query_place = jnp.arange(block_len)
-    causal = (key_slot[None, :] > 0) | (key_place[None, :] <= query_place[:, None])
-    visible = slot_open[:, :, None, None, :] & causal[None, None, None]
-    highest = jnp.max(jnp.where(visible, scores, -jnp.inf), axis=-1, keepdims=True)
-    weights = jnp.where(visible, jnp.exp(scores - highest), jnp.float32(0.0))
-    totals = jnp.sum(weights, axis=-1)
-    probabilities = weights.astype(jnp.bfloat16)
-    attended = jnp.einsum(
-        "egaqk,egkh->gqeah", probabilities, value_part, preferred_element_type=jnp.float32
-    )
-    scaled = attended / jnp.transpose(totals, (1, 3, 0, 2))[..., None]
-    return scaled.astype(jnp.bfloat16)
+NEGATIVE = -1e30
+
+
+def attend_kernel(index_ref, plain_ref, open_ref, side_ref, q_ref, k_ref, v_ref, o_ref, ka, va):
+    step = pl.program_id(0)
+    blocks = pl.num_programs(0)
+    rows_all, head_dim = q_ref.shape
+    block_len = k_ref.shape[2]
+    picks = ka.shape[0] // block_len
+    side_rows = side_ref.shape[1]
+    per_token = rows_all // block_len
+    factor = head_dim ** -0.5 * math.log2(math.e)
+    for s in range(picks):
+        for h in range(2):
+            place = index_ref[(h * blocks + step) * picks + s]
+            at = (slice(s * block_len, (s + 1) * block_len), slice(h * head_dim, (h + 1) * head_dim))
+            ka[at] = k_ref[h, place]
+            va[at] = v_ref[h, place]
+
+    def run(masked):
+        for c in range(rows_all // side_rows):
+            part = slice(c * side_rows, (c + 1) * side_rows)
+            q = q_ref[part, :]
+            qa = jnp.concatenate([q * side_ref[0], q * side_ref[1]], axis=1)
+            row = lax.broadcasted_iota(jnp.int32, (side_rows, block_len), 0)
+            lane = lax.broadcasted_iota(jnp.int32, (side_rows, block_len), 1)
+            first = lax.rem(row, per_token) < per_token // 2
+            token = lax.div(row, per_token) + c * (side_rows // per_token)
+            scores = lax.dot_general(
+                qa, ka[...], (((1,), (1,)), ((), ())), preferred_element_type=jnp.float32
+            )
+            parts = [scores[:, s * block_len : (s + 1) * block_len] for s in range(picks)]
+            parts[0] = jnp.where(lane <= token, parts[0], NEGATIVE)
+            if masked:
+                for s in range(1, picks):
+                    bias = [open_ref[(h * blocks + step) * picks + s] for h in range(2)]
+                    bias = jnp.where(first, bias[0], bias[1])
+                    parts[s] = jnp.where(bias > 0, parts[s], NEGATIVE)
+            top = parts[0]
+            for s in range(1, picks):
+                top = jnp.maximum(top, parts[s])
+            top = jnp.max(top, axis=1, keepdims=True)
+            weights = [jnp.exp2((x - top) * factor) for x in parts]
+            total = weights[0]
+            for s in range(1, picks):
+                total = total + weights[s]
+            total = jnp.sum(total, axis=1, keepdims=True)
+            probabilities = jnp.concatenate([w.astype(jnp.bfloat16) for w in weights], axis=1)
+            out = jnp.dot(probabilities, va[...], preferred_element_type=jnp.float32)
+            out = jnp.where(first, out[:, :head_dim], out[:, head_dim:])
+            o_ref[part, :] = (out * (1.0 / total)).astype(o_ref.dtype)
+
+    plain = plain_ref[step] > 0
+
+    @pl.when(plain)
+    def _():
+        run(False)
+
+    @pl.when(jnp.logical_not(plain))
+    def _():
+        run(True)
+
+
+SIDE_ROWS = 256
+
+
+def attend_all(queries, key_table, value_table, slot_index, slot_open):
+    tokens_dev, query_heads, head_dim = queries.shape
+    used_heads, table_blocks, block_len, _ = key_table.shape
+    blocks, picks = slot_index.shape[1:]
+    rows = block_len * query_heads
+    flat = queries.reshape(tokens_dev * query_heads, head_dim)
+    side = (jnp.arange(SIDE_ROWS) % query_heads < query_heads // 2)[None, :, None]
+    side = jnp.concatenate([side, ~side], axis=0).astype(jnp.bfloat16)
+    side = jnp.broadcast_to(side, (2, SIDE_ROWS, head_dim))
+    whole = lambda shape: pl.BlockSpec(shape, lambda b, *_: (0,) * len(shape), pipeline_mode=pl.Buffered(1))
+    plain = jnp.all(slot_open > 0, axis=(0, 2)).astype(jnp.int32)
+    out = pl.pallas_call(
+        attend_kernel,
+        out_shape=jax.ShapeDtypeStruct(flat.shape, jnp.bfloat16),
+        grid_spec=pltpu.PrefetchScalarGridSpec(
+            num_scalar_prefetch=3,
+            grid=(blocks,),
+            in_specs=[
+                whole(side.shape),
+                pl.BlockSpec((rows, head_dim), lambda b, *_: (b, 0)),
+                whole(key_table.shape),
+                whole(value_table.shape),
+            ],
+            out_specs=pl.BlockSpec((rows, head_dim), lambda b, *_: (b, 0)),
+            scratch_shapes=[
+                pltpu.VMEM((picks * block_len, 2 * head_dim), jnp.bfloat16),
+                pltpu.VMEM((picks * block_len, 2 * head_dim), jnp.bfloat16),
+            ],
+        ),
+        compiler_params=pltpu.CompilerParams(
+            dimension_semantics=("arbitrary",), vmem_limit_bytes=56 * 1024 * 1024
+        ),
+    )(slot_index.reshape(-1), plain, slot_open.reshape(-1), side, flat, key_table, value_table)
+    return out.reshape(tokens_dev, query_heads, head_dim)
 
 
 def on_device(queries, keys, values, chosen):
@@ -100,30 +179,10 @@
     slot_index = jnp.where(
         source == position, within, blocks + source * REMOTE_BLOCK_MAX + slot_rank
     )
-    group_size = 4
-    query_groups = queries.reshape(
-        blocks // group_size, group_size, block_len, used_heads, per_head, head_dim
-    )
-    index_groups = jnp.transpose(
-        slot_index.reshape(used_heads, blocks // group_size, group_size, picks), (1, 0, 2, 3)
-    )
-    chosen_groups = jnp.transpose(
-        chosen_used.reshape(used_heads, blocks // group_size, group_size, picks), (1, 0, 2, 3)
-    )
-    head_index = jnp.arange(used_heads, dtype=jnp.int32)[:, None, None]
-
-    def block_group(operands):
-        query_part, index_part, chosen_part = operands
-        key_part = key_table[head_index, index_part].reshape(
-            used_heads, group_size, picks * block_len, head_dim
-        )
-        value_part = value_table[head_index, index_part].reshape(
-            used_heads, group_size, picks * block_len, head_dim
-        )
-        return attend(query_part, key_part, value_part, chosen_part)
-
-    result = lax.map(block_group, (query_groups, index_groups, chosen_groups))
-    return result.reshape(tokens_dev, query_heads, head_dim)
+    before_slot = jnp.arange(picks)[:, None] > jnp.arange(picks)[None, :]
+    same = chosen_used[..., :, None] == chosen_used[..., None, :]
+    slot_open = jnp.logical_not(jnp.any(same & before_slot, axis=-1)).astype(jnp.int32)
+    return attend_all(queries, key_table, value_table, slot_index, slot_open)
 
 
 def solution(mesh):

time: 323 us -> 117 us (0.36)
  other arithmetic: 136 us -> 4.5 us
  matrix products: 81 us -> 0 us
  Pallas kernels: 0 us -> 58.3 us
  local copies, waits for them, and re-layouts: 72.9 us -> 23.1 us
    sub x6 -> x0, other arithmetic: 119 us -> none  [attend(): weights = jnp.where(visible, jnp.exp(scores - highest), jnp.float32(0.0))]
    dot_general x12 -> x0, matrix products: 81 us -> none  [the longest x6 48.4 us: attend(): jnp.einsum('gqeah,egkh->egaqk', query_part, key_part, preferred_element_t...]
    pallas_call x0 -> x1, Pallas kernels: none -> 58.3 us  [attend_all(): pl.pallas_call(attend_kernel, out_shape=jax.ShapeDtypeStruct(flat.shape,...]
    gather x12 -> x0, local copies, waits for them, and re-layouts: 28.4 us -> none  [the longest x6 15.3 us: block_group(): key_table[head_index, index_part]]
    dynamic_update_slice x12 -> x0, local copies, waits for them, and re-layouts: 12.3 us -> none  [on_device(): result = lax.map(block_group, (query_groups, index_groups, chosen_groups))]
    dynamic_slice x6 -> x0, local copies, waits for them, and re-layouts: 9.55 us -> none  [on_device(): result = lax.map(block_group, (query_groups, index_groups, chosen_groups))]
    and x6 -> x0, other arithmetic: 8.44 us -> none  [attend(): visible = slot_open[:, :, None, None, :] & causal[None, None, None]]
    transpose x1 -> x2, local copies, waits for them, and re-layouts: 0.2 us -> 6.44 us  [on_device(): jnp.transpose(fetch_values, (1, 0, 2))]
  transfers between devices with their start and end apart: 3 -> 3, of which waited for: 2 -> 2; matrix products, arithmetic and copies ran while one was open for 6% -> 17% of each run, Pallas kernels for 0% -> 0%
where the time goes in v1:
time: 117 us; the launch traced here: 116 us
  Pallas kernels  58.3 us (50%)
  local copies, waits for them, and re-layouts  23.1 us (20%)
  starting transfers between devices  15.6 us (13%)
  waiting for transfers between devices  14.5 us (12%)
  other arithmetic  4.5 us (4%)
    pallas_call x1, Pallas kernels, attend_all(): pl.pallas_call(attend_kernel, out_shape=jax.ShapeDtypeStruct(flat.shape,...  58.3 us
    all_to_all x1, waiting for transfers between devices, on_device(): lax.all_to_all(send_values, 'ctx', split_axis=1, concat_axis=1, tiled=True)  8.3 us
    transpose x2, local copies, waits for them, and re-layouts, on_device(): jnp.transpose(fetch_values, (1, 0, 2))  6.44 us
    all_to_all x1, starting transfers between devices, on_device(): lax.all_to_all(request, 'ctx', split_axis=1, concat_axis=1, tiled=True)  6.35 us
    all_to_all x1, waiting for transfers between devices, on_device(): lax.all_to_all(send_keys, 'ctx', split_axis=1, concat_axis=1, tiled=True)  6.15 us
    all_to_all x1, starting transfers between devices, on_device(): lax.all_to_all(send_values, 'ctx', split_axis=1, concat_axis=1, tiled=True)  5.09 us
    all_to_all x1, starting transfers between devices, on_device(): lax.all_to_all(send_keys, 'ctx', split_axis=1, concat_axis=1, tiled=True)  4.13 us
    gather x4, local copies, waits for them, and re-layouts, on_device(): jnp.take_along_axis(rank_used, chosen_used.reshape(used_heads, blocks * p...  3.77 us
  transfers between devices with their start and end apart: 3, of which 2 were waited for; matrix products, arithmetic and copies ran while one was open for 17% of the time, Pallas kernels for 0%

profile of v1, /device:TPU:0, one launch (start us, length us, event | category | flops | bytes accessed | tf_op | source)
XLA Modules:
  0.0 116.1 jit_solution(11197222754563634435)
XLA Ops:
  0.0 0.7 constant_dynamic-slice_fusion
  0.8 0.1 eq.53
  0.9 0.1 fusion
  1.0 0.1 reshape.158
  1.2 0.4 reduce_window_sum.11
  1.6 0.2 select_reduce_fusion
  1.7 0.7 copy.29
  2.4 6.3 %all-to-all-start = ((s32[2,4,2]{2,0,1:T(2,128)}), s32[2,4,2]{2,0,1:T(2,128)S(1)}, u32[]{:S(2)}, u32[]{:S(2)}) async-start(s32[2,4,2]{2,0,1:T(2,128)} %copy.29), calls=%async_computation | async-start | bytes 8192 | tf_op jit(solution)/shard_map/all_to_all | solution.py:149
  8.8 6.2 %dynamic-slice_bitcast_fusion = (bf16[2,3072,128]{2,0,1:T(2,128)(2,1)S(1)}, bf16[2,3072,128]{2,0,1:T(2,128)(2,1)}) fusion(bf16[3072,4,128]{2,1,0:T(4,128)(2,1)} %param.6, s32[]{:T(128)S(6)} %select_n.77, bf16[3072,4,128]{2,1,0:T(4,128)(2,1)} %param.5), kind=kLoop, calls=%fused_computation.5 | loop fusion | bytes 6291460 | tf_op jit(solution)/shard_map/transpose | solution.py:153
  15.0 0.2 copy.34
  15.2 0.1 copy.30
  15.4 0.1 copy.31
  15.5 0.7 gather_fusion.1
  16.2 0.8 copy.35
  17.0 5.1 %all-to-all-start.2 = ((bf16[2,4,256,128]{3,2,0,1:T(8,128)(2,1)}), bf16[2,4,256,128]{3,2,0,1:T(8,128)(2,1)}, u32[]{:S(2)}, u32[]{:S(2)}) async-start(bf16[2,4,256,128]{3,2,0,1:T(8,128)(2,1)} %copy.35), calls=%async_computation.2 | async-start | bytes 1048576 | tf_op jit(solution)/shard_map/all_to_all | solution.py:165
  22.3 0.1 and_reduce_fusion
  22.4 0.5 convert_element_type.26.plain_ref
  23.0 1.6 %copy.28 = bf16[2,3072,128]{2,1,0:T(8,128)(2,1)S(1)} copy(bf16[2,3072,128]{2,0,1:T(2,128)(2,1)} %get-tuple-element.12) | data formatting | bytes 3145728 | tf_op jit(solution)/shard_map/transpose | solution.py:150
  24.6 1.4 %gather_fusion = bf16[16,128,128]{2,1,0:T(8,128)(2,1)} fusion(bf16[2,24,128,128]{3,2,1,0:T(8,128)(2,1)S(1)} %bitcast.20, s32[16]{0:T(128)S(1)} %reshape.170), kind=kCustom, calls=%fused_computation | custom fusion | bytes 1048704 | tf_op jit(solution)/shard_map/gather | solution.py:157
  26.0 1.9 %copy.32 = bf16[2,4,256,128]{3,2,0,1:T(8,128)(2,1)} copy(bf16[2,4,256,128]{3,2,1,0:T(8,128)(2,1)} %bitcast.23) | data formatting | bytes 1048576 | tf_op jit(solution)/shard_map/reshape | solution.py:157
  27.9 8.3 %all-to-all-done.2 = bf16[2,4,256,128]{3,2,0,1:T(8,128)(2,1)} async-done(((bf16[2,4,256,128]{3,2,0,1:T(8,128)(2,1)}), bf16[2,4,256,128]{3,2,0,1:T(8,128)(2,1)}, u32[]{:S(2)}, u32[]{:S(2)}) %all-to-all-start.2) | async-done | bytes 524320 | tf_op jit(solution)/shard_map/all_to_all | solution.py:165
  36.2 4.1 %all-to-all-start.1 = ((bf16[2,4,256,128]{3,2,0,1:T(8,128)(2,1)}), bf16[2,4,256,128]{3,2,0,1:T(8,128)(2,1)}, u32[]{:S(2)}, u32[]{:S(2)}) async-start(bf16[2,4,256,128]{3,2,0,1:T(8,128)(2,1)} %copy.32), calls=%async_computation.1 | async-start | bytes 1048576 | tf_op jit(solution)/shard_map/all_to_all | solution.py:164
  40.5 0.7 reshape.169.open_ref
  41.1 3.5 %gather_fusion.2 = s32[384]{0:T(512)S(1)} fusion(s32[2,96]{1,0:T(2,128)S(1)} %sub.19, s32[384]{0:T(512)S(1)} %reshape.182), kind=kCustom, calls=%fused_computation.2 | custom fusion | bytes 6144 | tf_op jit(solution)/shard_map/jit(take_along_axis)/gather | solution.py:176
  45.0 0.7 reshape.160.index_ref
  45.7 1.1 copy.36
  46.7 1.5 %pad_maximum_fusion.1.v_ref = bf16[2,32,128,128]{3,2,1,0:T(8,128)(2,1)} fusion(bf16[2,8,128,128]{3,2,1,0:T(8,128)(2,1)S(1)} %bitcast.25, bf16[2,24,128,128]{3,2,1,0:T(8,128)(2,1)S(1)} %bitcast.19), kind=kLoop, calls=%fused_computation.4 | loop fusion | flops 1048576 | bytes 4194304 | tf_op jit(solution)/shard_map/concatenate | solution.py:173
  48.3 6.2 %all-to-all-done.1 = bf16[2,4,256,128]{3,2,0,1:T(8,128)(2,1)} async-done(((bf16[2,4,256,128]{3,2,0,1:T(8,128)(2,1)}), bf16[2,4,256,128]{3,2,0,1:T(8,128)(2,1)}, u32[]{:S(2)}, u32[]{:S(2)}) %all-to-all-start.1) | async-done | bytes 524320 | tf_op jit(solution)/shard_map/all_to_all | solution.py:164
  54.4 1.1 copy.33
  55.5 1.5 %pad_maximum_fusion.k_ref = bf16[2,32,128,128]{3,2,1,0:T(8,128)(2,1)} fusion(bf16[2,8,128,128]{3,2,1,0:T(8,128)(2,1)S(1)} %bitcast.26, bf16[2,24,128,128]{3,2,1,0:T(8,128)(2,1)S(1)} %bitcast.21), kind=kLoop, calls=%fused_computation.3 | loop fusion | flops 1048576 | bytes 4194304 | tf_op jit(solution)/shard_map/concatenate | solution.py:172
  57.0 0.8 broadcast_in_dim.10.side_ref
  57.8 58.3 %shard_map.46 = bf16[24576,128]{1,0:T(8,128)(2,1)} custom-call(s32[384]{0:T(512)} %reshape.160.index_ref, s32[24]{0:T(128)} %convert_element_type.26.plain_ref, s32[384]{0:T(512)} %reshape.169.open_ref, bf16[2,256,128]{2,1,0:T(8,128)(2,1)} %broadcast_in_dim.10.side_ref, bf16[24576,128]{1,0:T(8,128)(2,1)} %bitcast.22, ...), custom_call_target="tpu_custom_call" | custom-call | tf_op jit(solution)/shard_map/pallas_call | solution.py:92
  (23 shorter events, 0.9 us)
Async XLA Ops:
  2.4 12.8 %all-to-all-start = ((s32[2,4,2]{2,0,1:T(2,128)}), s32[2,4,2]{2,0,1:T(2,128)S(1)}, u32[]{:S(2)}, u32[]{:S(2)}) async-start(s32[2,4,2]{2,0,1:T(2,128)} %copy.29), calls=%async_computation | async-start | bytes 8192 | tf_op jit(solution)/shard_map/all_to_all | solution.py:149
  17.0 19.1 %all-to-all-start.2 = ((bf16[2,4,256,128]{3,2,0,1:T(8,128)(2,1)}), bf16[2,4,256,128]{3,2,0,1:T(8,128)(2,1)}, u32[]{:S(2)}, u32[]{:S(2)}) async-start(bf16[2,4,256,128]{3,2,0,1:T(8,128)(2,1)} %copy.35), calls=%async_computation.2 | async-start | bytes 1048576 | tf_op jit(solution)/shard_map/all_to_all | solution.py:165
  26.0 18.9 %copy-start = (s32[4,24,8]{1,2,0:T(8,128)S(1)}, s32[4,24,8]{1,2,0:T(8,128)}, u32[]{:S(2)}) copy-start(s32[4,24,8]{1,2,0:T(8,128)} %param.7) | copy-start | bytes 9220
  36.2 18.2 %all-to-all-start.1 = ((bf16[2,4,256,128]{3,2,0,1:T(8,128)(2,1)}), bf16[2,4,256,128]{3,2,0,1:T(8,128)(2,1)}, u32[]{:S(2)}, u32[]{:S(2)}) async-start(bf16[2,4,256,128]{3,2,0,1:T(8,128)(2,1)} %copy.32), calls=%async_computation.1 | async-start | bytes 1048576 | tf_op jit(solution)/shard_map/all_to_all | solution.py:164

commit v2 on v0

v2 whole, which is shorter than its diff:
```python
import functools
import math

import jax
import jax.numpy as jnp
from jax import lax
from jax.experimental import pallas as pl
from jax.experimental.pallas import tpu as pltpu
from jax.sharding import PartitionSpec as P

QUERY_HEADS = 32
KEY_VALUE_HEADS = 8
REMOTE_BLOCK_MAX = 2
NEGATIVE = -1e30
BIG = 1 << 30
SIDE_ROWS = 256
PLAN_ROWS = 16
MESH = pl.DeviceIdType.MESH


def prepare_kernel(shards, query_heads, chosen_ref, k_hbm, v_hbm, *refs):
    plan_ref, kt_ref, vt_ref = refs[:3]
    send_refs = refs[3 : 3 + shards - 1]
    raw, ask, asked, asked_s, load_sem, send_sem, recv_sem, move_sem = refs[3 + shards - 1 :]
    me = lax.axis_index("ctx")
    heads, blocks, block_len, head_dim = kt_ref.shape
    first_head = lax.axis_index("rep") * query_heads // (QUERY_HEADS // KEY_VALUE_HEADS)
    kv_heads, picks, _ = chosen_ref.shape
    loads = [pltpu.make_async_copy(src, raw.at[i], load_sem.at[i]) for i, src in enumerate((k_hbm, v_hbm))]
    for load in loads:
        load.start()
    barrier = pltpu.get_barrier_semaphore()
    for d in range(1, shards):
        pl.semaphore_signal(barrier, inc=1, device_id={"ctx": lax.rem(me + d, shards)}, device_id_type=MESH)

    lane = lax.broadcasted_iota(jnp.int32, (8, 128), 1)
    tiles = [jnp.zeros((8, 128), jnp.int32) for _ in range(1, shards)]
    for h in range(heads):
        chosen = chosen_ref[first_head + h]
        base = me * blocks
        local = (chosen >= base) & (chosen < base + blocks)
        slot = jnp.where(local, chosen - base, 0)
        for d in range(1, shards):
            start = (me - d) * blocks
            inside = (chosen >= start) & (chosen < start + blocks)
            first = jnp.min(jnp.where(inside, chosen, BIG), keepdims=True)
            later = inside & (chosen > first)
            second = jnp.min(jnp.where(later, chosen, BIG), keepdims=True)
            slot = jnp.where(inside, blocks + (d - 1) * 2 * heads + later.astype(jnp.int32), slot)
            for r, place in enumerate((first, second)):
                place = jnp.clip(place - start, 0, blocks - 1)
                tiles[d - 1] = jnp.where(lane == h * 2 + r, place, tiles[d - 1])
        rows = [chosen[k : k + 1, :] for k in range(picks)]
        slots = [slot[k : k + 1, :] for k in range(picks)]
        near = [(x >= base) & (x < base + blocks) for x in rows]
        is_local, is_remote = [], []
        for k in range(picks):
            fresh = jnp.ones(rows[k].shape, jnp.int32)
            for j in range(k):
                fresh = jnp.where(rows[j] == rows[k], 0, fresh)
            is_local.append(jnp.where(near[k], fresh, 0))
            is_remote.append(jnp.where(near[k], 0, fresh))
        local_count = functools.reduce(jnp.add, is_local)
        place_of, at_local, at_remote = [], jnp.zeros_like(local_count), local_count
        for k in range(picks):
            place = jnp.where(is_local[k] > 0, at_local, at_remote)
            place_of.append(jnp.where(is_local[k] + is_remote[k] > 0, place, picks))
            at_local = at_local + is_local[k]
            at_remote = at_remote + is_remote[k]
        for p in range(picks):
            total = jnp.zeros_like(local_count)
            for k in range(picks):
                total = jnp.where(place_of[k] == p, slots[k], total)
            plan_ref[h * PLAN_ROWS + p : h * PLAN_ROWS + p + 1, :] = total
        plan_ref[h * PLAN_ROWS + picks : h * PLAN_ROWS + picks + 1, :] = local_count
        plan_ref[h * PLAN_ROWS + picks + 1 : h * PLAN_ROWS + picks + 2, :] = at_remote
        for p in range(picks + 2, PLAN_ROWS):
            plan_ref[h * PLAN_ROWS + p : h * PLAN_ROWS + p + 1, :] = jnp.zeros_like(local_count)
    for d in range(1, shards):
        ask[d - 1] = tiles[d - 1]
    pl.semaphore_wait(barrier, shards - 1)

    def request(d):
        return pltpu.make_async_remote_copy(
            src_ref=ask.at[d - 1],
            dst_ref=asked.at[d - 1],
            send_sem=send_sem.at[d - 1],
            recv_sem=recv_sem.at[d - 1],
            device_id={"ctx": lax.rem(me - d + shards, shards)},
            device_id_type=MESH,
        )

    for d in range(1, shards):

        @pl.when(me >= d)
        def _(d=d):
            request(d).start()

    for load in loads:
        load.wait()
    wide = kv_heads * block_len
    out_row = lax.broadcasted_iota(jnp.int32, (heads * block_len, wide), 0)
    in_row = lax.broadcasted_iota(jnp.int32, (heads * block_len, wide), 1)
    source = lax.rem(out_row, block_len) * kv_heads + first_head + lax.div(out_row, block_len)
    pick = jnp.where(source == in_row, 1.0, 0.0).astype(jnp.bfloat16)

    def split(b, carry):
        rows = pl.ds(pl.multiple_of(b * wide, wide), wide)
        for i, table in enumerate((kt_ref, vt_ref)):
            parted = jnp.dot(pick, raw[i, rows, :], preferred_element_type=jnp.float32).astype(jnp.bfloat16)
            for h in range(heads):
                table[h, b] = parted[h * block_len : (h + 1) * block_len, :]
        return carry

    lax.fori_loop(0, blocks, split, 0)
    for d in range(1, shards):

        @pl.when(me + d < shards)
        def _(d=d):
            request(d).wait_recv()
            move = pltpu.make_async_copy(asked.at[d - 1], asked_s.at[d - 1], move_sem.at[d - 1])
            move.start()
            move.wait()
            for h in range(heads):
                for r in range(2):
                    place = asked_s[d - 1, 0, h * 2 + r]
                    for i, table in enumerate((kt_ref, vt_ref)):
                        send_refs[d - 1][i, h * 2 + r] = table[h, place]

    for d in range(1, shards):

        @pl.when(me >= d)
        def _(d=d):
            request(d).wait_send()


def prepare(chosen, keys, values, shards, query_heads):
    kv_heads, picks, blocks = chosen.shape
    tokens, _, head_dim = keys.shape
    block_len = tokens // blocks
    heads = max(1, query_heads // (QUERY_HEADS // KEY_VALUE_HEADS))
    vmem = pl.BlockSpec(memory_space=pltpu.VMEM)
    table = jax.ShapeDtypeStruct((heads, blocks, block_len, head_dim), jnp.bfloat16)
    sent = jax.ShapeDtypeStruct((2, heads * 2, block_len, head_dim), jnp.bfloat16)
    partners = shards - 1
    return pl.pallas_call(
        functools.partial(prepare_kernel, shards, query_heads),
        out_shape=[jax.ShapeDtypeStruct((heads * PLAN_ROWS, blocks), jnp.int32), table, table] + [sent] * partners,
        in_specs=[vmem, pl.BlockSpec(memory_space=pl.ANY), pl.BlockSpec(memory_space=pl.ANY)],
        out_specs=[vmem] * (3 + partners),
        scratch_shapes=[
            pltpu.VMEM((2, tokens * kv_heads, head_dim), jnp.bfloat16),
            pltpu.VMEM((partners, 8, 128), jnp.int32),
            pltpu.VMEM((partners, 8, 128), jnp.int32),
            pltpu.SMEM((partners, 8, 128), jnp.int32),
            pltpu.SemaphoreType.DMA((2,)),
            pltpu.SemaphoreType.DMA((partners,)),
            pltpu.SemaphoreType.DMA((partners,)),
            pltpu.SemaphoreType.DMA((partners,)),
        ],
        compiler_params=pltpu.CompilerParams(
            collective_id=0, has_side_effects=True, vmem_limit_bytes=48 * 1024 * 1024
        ),
    )(chosen, keys.reshape(-1, head_dim), values.reshape(-1, head_dim))


def attend_step(heads, plan_ref, remote, picks, side_ref, q_ref, read, ka, va, finish):
    step = pl.program_id(0)
    rows_all, head_dim = q_ref.shape
    block_len = ka.shape[0] // picks
    per_token = rows_all // block_len
    shape = (SIDE_ROWS // 8, 8, head_dim)
    factor = head_dim ** -0.5 * math.log2(math.e)
    local = [plan_ref[h * PLAN_ROWS + picks, step] for h in range(heads)]
    every = [plan_ref[h * PLAN_ROWS + picks + 1, step] for h in range(heads)]
    start = local if remote else [0] * heads
    count = [every[h] - local[h] for h in range(heads)] if remote else local
    most = functools.reduce(jnp.maximum, count)

    def body(n):
        for s in range(n):
            for h in range(heads):
                spot = jnp.where(s < count[h], jnp.minimum(start[h] + s, picks - 1), start[h])
                spot = jnp.where(count[h] > 0, spot, 0)
                place = plan_ref[h * PLAN_ROWS + spot, step]
                at = (slice(s * block_len, (s + 1) * block_len), slice(h * head_dim, (h + 1) * head_dim))
                ka[at], va[at] = read(h, jnp.where(count[h] > 0, place, -1))
        low = lax.rem(lax.broadcasted_iota(jnp.int32, (1, 8, head_dim), 1), per_token) < per_token // 2
        bias = []
        for s in range(n):
            side_bias = [jnp.where(s < count[h], 0.0, NEGATIVE) for h in range(heads)]
            bias.append(jnp.where(low, side_bias[0], side_bias[-1]))
        row = lax.broadcasted_iota(jnp.int32, (SIDE_ROWS // 8, 8, block_len), 0)
        if per_token != 8:
            row = lax.div(row * 8 + lax.broadcasted_iota(jnp.int32, row.shape, 1), per_token)
        lane = lax.broadcasted_iota(jnp.int32, row.shape, 2)
        for c in range(rows_all // SIDE_ROWS):
            part = slice(c * SIDE_ROWS, (c + 1) * SIDE_ROWS)
            if n == 0:
                finish(part, None, None, None)
                continue
            q = q_ref[part, :]
            qa = q if heads == 1 else jnp.concatenate([q * side_ref[0], q * side_ref[1]], axis=1)
            scores = lax.dot_general(
                qa, ka[: n * block_len, :], (((1,), (1,)), ((), ())), preferred_element_type=jnp.float32
            )
            parts = [
                scores[:, s * block_len : (s + 1) * block_len].reshape(row.shape)
                for s in range(n)
            ]
            for s in range(n):
                if s == 0 and not remote:
                    parts[s] = jnp.where(lane <= row + c * (SIDE_ROWS // per_token), parts[s], NEGATIVE)
                else:
                    parts[s] = parts[s] + bias[s]
            top = functools.reduce(jnp.maximum, parts)
            top = jnp.max(top, axis=2, keepdims=True)
            weights = [jnp.exp2((x - top) * factor) for x in parts]
            total = jnp.sum(functools.reduce(jnp.add, weights), axis=2, keepdims=True)
            probabilities = jnp.concatenate(
                [w.reshape(SIDE_ROWS, block_len).astype(jnp.bfloat16) for w in weights], axis=1
            )
            out = jnp.dot(probabilities, va[: n * block_len, :], preferred_element_type=jnp.float32)
            if heads == 1:
                out = out.reshape(shape)
            else:
                out = jnp.where(low, out[:, :head_dim].reshape(shape), out[:, head_dim:].reshape(shape))
            finish(part, top, total, out)

    for n in range(0 if remote else 1, picks if remote else picks + 1):
        pl.when(most == n)(functools.partial(body, n))


def local_kernel(heads, picks, plan_ref, side_ref, q_ref, k_ref, v_ref, sum_ref, stat_ref, ka, va):
    head_dim = q_ref.shape[1]

    def read(h, place):
        place = jnp.maximum(place, 0)
        return k_ref[h, place], v_ref[h, place]

    def finish(part, top, total, out):
        half = lax.broadcasted_iota(jnp.int32, (1, 1, head_dim), 2) < head_dim // 2
        sum_ref[part, :] = out.reshape(-1, head_dim)
        stat_ref[part, :] = jnp.where(half, top, total).reshape(-1, head_dim)

    attend_step(heads, plan_ref, False, picks, side_ref, q_ref, read, ka, va, finish)


def remote_kernel(heads, picks, blocks, plan_ref, side_ref, q_ref, sum_ref, stat_ref, *refs):
    o_ref, table, ka, va, sem = refs[-5:]
    arrived = refs[:-5]
    rows_all, head_dim = q_ref.shape
    factor = head_dim ** -0.5 * math.log2(math.e)

    @pl.when(pl.program_id(0) == 0)
    def _():
        copies = [
            pltpu.make_async_copy(ref.at[i], table.at[i, pl.ds(2 * heads * d, 2 * heads)], sem.at[d, i])
            for d, ref in enumerate(arrived)
            for i in range(2)
        ]
        for copy in copies:
            copy.start()
        for copy in copies:
            copy.wait()

    def read(h, place):
        place = jnp.maximum(place - blocks, 0) + h * 2
        return table[0, place], table[1, place]

    def finish(part, top, total, out):
        shape = (-1, 8, head_dim)
        stat = stat_ref[part, :].reshape(shape)
        near_top, near_total = stat[:, :, :1], stat[:, :, head_dim - 1 :]
        near = sum_ref[part, :].reshape(shape)
        if top is not None:
            new_top = jnp.maximum(top, near_top)
            keep, add = jnp.exp2((near_top - new_top) * factor), jnp.exp2((top - new_top) * factor)
            near = near * keep + out * add
            near_total = near_total * keep + total * add
        near = near * (1.0 / near_total)
        o_ref[part, :] = near.reshape(-1, head_dim).astype(o_ref.dtype)

    attend_step(heads, plan_ref, True, picks, side_ref, q_ref, read, ka, va, finish)


def on_device(queries, keys, values, chosen):
    tokens_dev, query_heads, head_dim = queries.shape
    kv_heads, blocks, picks = chosen.shape
    block_len = tokens_dev // blocks
    shards = lax.axis_size("ctx")
    plan, key_table, value_table, *sent = prepare(jnp.transpose(chosen, (0, 2, 1)), keys, values, shards, query_heads)
    arrived = [
        lax.ppermute(block, "ctx", [(i, i + d) for i in range(shards - d)])
        for d, block in enumerate(sent, 1)
    ]
    rows = block_len * query_heads
    heads = key_table.shape[0]
    flat = queries.reshape(tokens_dev * query_heads, head_dim)
    side = (jnp.arange(SIDE_ROWS) % query_heads < query_heads // 2)[None, :, None]
    side = jnp.concatenate([side, ~side], axis=0).astype(jnp.bfloat16)
    side = jnp.broadcast_to(side, (2, SIDE_ROWS, head_dim))
    whole = lambda x: pl.BlockSpec(x.shape, lambda b, *_: (0,) * x.ndim, pipeline_mode=pl.Buffered(1))
    tile = pl.BlockSpec((rows, head_dim), lambda b, *_: (b, 0))
    pair = [pltpu.VMEM((picks * block_len, heads * head_dim), jnp.bfloat16)] * 2
    params = pltpu.CompilerParams(dimension_semantics=("arbitrary",), vmem_limit_bytes=48 * 1024 * 1024)
    cost = pl.CostEstimate(
        flops=4 * flat.size * picks * block_len, bytes_accessed=12 * flat.size, transcendentals=0
    )
    partial_sum, stat = pl.pallas_call(
        functools.partial(local_kernel, heads, picks),
        out_shape=[jax.ShapeDtypeStruct(flat.shape, jnp.float32)] * 2,
        grid_spec=pltpu.PrefetchScalarGridSpec(
            num_scalar_prefetch=1,
            grid=(blocks,),
            in_specs=[whole(side), tile, whole(key_table), whole(value_table)],
            out_specs=[tile, tile],
            scratch_shapes=pair,
        ),
        compiler_params=params,
        cost_estimate=cost,
    )(plan, side, flat, key_table, value_table)
    out = pl.pallas_call(
        functools.partial(remote_kernel, heads, picks, blocks),
        out_shape=jax.ShapeDtypeStruct(flat.shape, jnp.bfloat16),
        grid_spec=pltpu.PrefetchScalarGridSpec(
            num_scalar_prefetch=1,
            grid=(blocks,),
            in_specs=[whole(side), tile, tile, tile] + [pl.BlockSpec(memory_space=pl.ANY)] * len(arrived),
            out_specs=tile,
            scratch_shapes=[
                pltpu.VMEM((2, 2 * heads * len(arrived), block_len, head_dim), jnp.bfloat16),
                *pair,
                pltpu.SemaphoreType.DMA((len(arrived), 2)),
            ],
        ),
        compiler_params=params,
        cost_estimate=cost,
    )(plan, side, flat, partial_sum, stat, *arrived)
    return out.reshape(tokens_dev, query_heads, head_dim)


def solution(mesh):
    placed = (
        P(("groups", "ctx"), ("heads", "rep"), None),
        P(("groups", "ctx"), "heads", None),
        P(("groups", "ctx"), "heads", None),
        P("heads", ("groups", "ctx"), None),
    )
    return jax.shard_map(
        on_device,
        mesh=mesh,
        in_specs=placed,
        out_specs=P(("groups", "ctx"), ("heads", "rep"), None),
        check_vma=False,
    )
```

time: 323 us -> 146 us (0.45)
  the two profiles are of different devices: /device:TPU:0 before, /device:TPU:26 now
where the time goes in v2:
time: 146 us; the launch traced here: 145 us
  Pallas kernels  140 us (96%)
  starting transfers between devices  3.88 us (3%)
    pallas_call x1, Pallas kernels, on_device(): pl.pallas_call(functools.partial(remote_kernel, heads, picks, blocks), ou...  90.7 us
    pallas_call x1, Pallas kernels, on_device(): pl.pallas_call(functools.partial(local_kernel, heads, picks), out_shape=[...  39.7 us
    pallas_call x1, Pallas kernels, prepare(): pl.pallas_call(functools.partial(prepare_kernel, shards, query_heads), ou...  10 us
    ppermute x3, starting transfers between devices, on_device(): lax.ppermute(block, 'ctx', [(i, i + d) for i in range(shards - d)])  3.88 us
  transfers between devices with their start and end apart: 3, of which 0 were waited for; matrix products, arithmetic and copies ran while one was open for 0% of the time, Pallas kernels for 27%

profile of v2, /device:TPU:26, one launch (start us, length us, event | category | flops | bytes accessed | tf_op | source)
XLA Modules:
  0.0 145.4 jit_solution(11040686924311696524)
XLA Ops:
  0.0 0.0 copy-start
  0.0 0.7 copy-done
  0.7 10.0 %shard_map.46 = (s32[32,24]{1,0:T(8,128)S(1)}, bf16[2,24,128,128]{3,2,1,0:T(8,128)(2,1)S(1)}, bf16[2,24,128,128]{3,2,1,0:T(8,128)(2,1)S(1)}, bf16[2,4,128,128]{3...) custom-call(s32[4,8,24]{2,1,0:T(8,128)S(1)} %bitcast.5, ...), custom_call_target="tpu_custom_call" | custom-call | tf_op jit(solution)/shard_map/pallas_call | solution.py:146
  10.8 1.3 collective-permute-start
  12.1 1.3 collective-permute-start.1
  13.4 1.3 collective-permute-start.2
  14.7 0.1 broadcast_in_dim.2.side_ref
  14.8 39.7 %shard_map.47 = (f32[24576,128]{1,0:T(8,128)}, f32[24576,128]{1,0:T(8,128)}) custom-call(s32[32,24]{1,0:T(8,128)S(1)} %get-tuple-element.13.plan_ref, bf16[2,256,128]{2,1,0:T(8,128)(2,1)S(1)} %broadcast_in_dim.2.side_ref, bf16[24576,128]{1,0:T(8,128)(2,1)} %bitcast.8, bf16[2,24,128,128]{3,2,1,0:T(8,128)(2,1)S(1)} %get-tuple-element.14.k_ref, ...), custom_call_target="tpu_custom_call" | custom-call | flops 12884901888 | bytes 37748736 | tf_op jit(solution)/shard_map/pallas_call | solution.py:310
  54.5 0.0 collective-permute-done.refs_0_
  54.5 0.0 collective-permute-done.1.refs_1_
  54.5 0.0 collective-permute-done.2.refs_2_
  54.6 90.7 %shard_map.48 = bf16[24576,128]{1,0:T(8,128)(2,1)} custom-call(s32[32,24]{1,0:T(8,128)S(1)} %get-tuple-element.13.plan_ref, bf16[2,256,128]{2,1,0:T(8,128)(2,1)S(1)} %broadcast_in_dim.2.side_ref, bf16[24576,128]{1,0:T(8,128)(2,1)} %bitcast.9, f32[24576,128]{1,0:T(8,128)} %get-tuple-element.16.sum_ref, f32[24576,128]{1,0:T(8,128)} %get-tuple-element.17.stat_ref, ...), custom_call_target="tpu_custom_call" | custom-call | flops 12884901888 | bytes 37748736 | tf_op jit(solution)/shard_map/pallas_call | solution.py:323
  (2 shorter events, 0.0 us)
Async XLA Ops:
  0.0 0.7 copy-start
  10.8 43.8 %collective-permute-start = (bf16[2,4,128,128]{3,2,1,0:T(8,128)(2,1)S(1)}, bf16[2,4,128,128]{3,2,1,0:T(8,128)(2,1)S(1)}, u32[]{:S(2)}, u32[]{:S(2)}) collective-permute-start(bf16[2,4,128,128]{3,2,1,0:T(8,128)(2,1)S(1)} %get-tuple-element.18), channel_id=1, source_target_pairs={{0,4},{4,8},{8,12},{1,5},{5,9},{9,13},{2,6},{6,10},{10,14},{3,7},{... | collective-permute-start | bytes 786440 | tf_op jit(solution)/shard_map/ppermute | solution.py:294
  12.1 42.5 %collective-permute-start.1 = (bf16[2,4,128,128]{3,2,1,0:T(8,128)(2,1)S(1)}, bf16[2,4,128,128]{3,2,1,0:T(8,128)(2,1)S(1)}, u32[]{:S(2)}, u32[]{:S(2)}) collective-permute-start(bf16[2,4,128,128]{3,2,1,0:T(8,128)(2,1)S(1)} %get-tuple-element.19), channel_id=1, source_target_pairs={{0,8},{4,12},{1,9},{5,13},{2,10},{6,14},{3,11},{7,15},{16,24},{20,... | collective-permute-start | bytes 786440 | tf_op jit(solution)/shard_map/ppermute | solution.py:294
  13.4 41.2 %collective-permute-start.2 = (bf16[2,4,128,128]{3,2,1,0:T(8,128)(2,1)S(1)}, bf16[2,4,128,128]{3,2,1,0:T(8,128)(2,1)S(1)}, u32[]{:S(2)}, u32[]{:S(2)}) collective-permute-start(bf16[2,4,128,128]{3,2,1,0:T(8,128)(2,1)S(1)} %get-tuple-element.20), channel_id=1, source_target_pairs={{0,12},{1,13},{2,14},{3,15},{16,28},{17,29},{18,30},{19,31}} | collective-permute-start | bytes 786440 | tf_op jit(solution)/shard_map/ppermute | solution.py:294

commit v3 on v2

--- a/solution.py
+++ b/solution.py
@@ -231,7 +231,7 @@
         pl.when(most == n)(functools.partial(body, n))
 
 
-def local_kernel(heads, picks, plan_ref, side_ref, q_ref, k_ref, v_ref, sum_ref, stat_ref, ka, va):
+def local_kernel(heads, picks, plan_ref, side_ref, q_ref, k_ref, v_ref, sum_ref, top_ref, total_ref, ka, va):
     head_dim = q_ref.shape[1]
 
     def read(h, place):
@@ -239,14 +239,14 @@
         return k_ref[h, place], v_ref[h, place]
 
     def finish(part, top, total, out):
-        half = lax.broadcasted_iota(jnp.int32, (1, 1, head_dim), 2) < head_dim // 2
         sum_ref[part, :] = out.reshape(-1, head_dim)
-        stat_ref[part, :] = jnp.where(half, top, total).reshape(-1, head_dim)
+        top_ref[part, :] = jnp.broadcast_to(top, out.shape).reshape(-1, head_dim)
+        total_ref[part, :] = jnp.broadcast_to(total, out.shape).reshape(-1, head_dim)
 
     attend_step(heads, plan_ref, False, picks, side_ref, q_ref, read, ka, va, finish)
 
 
-def remote_kernel(heads, picks, blocks, plan_ref, side_ref, q_ref, sum_ref, stat_ref, *refs):
+def remote_kernel(heads, picks, blocks, plan_ref, side_ref, q_ref, sum_ref, top_ref, total_ref, *refs):
     o_ref, table, ka, va, sem = refs[-5:]
     arrived = refs[:-5]
     rows_all, head_dim = q_ref.shape
@@ -270,8 +270,7 @@
 
     def finish(part, top, total, out):
         shape = (-1, 8, head_dim)
-        stat = stat_ref[part, :].reshape(shape)
-        near_top, near_total = stat[:, :, :1], stat[:, :, head_dim - 1 :]
+        near_top, near_total = top_ref[part, :].reshape(shape), total_ref[part, :].reshape(shape)
         near = sum_ref[part, :].reshape(shape)
         if top is not None:
             new_top = jnp.maximum(top, near_top)
@@ -307,14 +306,14 @@
     cost = pl.CostEstimate(
         flops=4 * flat.size * picks * block_len, bytes_accessed=12 * flat.size, transcendentals=0
     )
-    partial_sum, stat = pl.pallas_call(
+    partials = pl.pallas_call(
         functools.partial(local_kernel, heads, picks),
-        out_shape=[jax.ShapeDtypeStruct(flat.shape, jnp.float32)] * 2,
+        out_shape=[jax.ShapeDtypeStruct(flat.shape, jnp.float32)] * 3,
         grid_spec=pltpu.PrefetchScalarGridSpec(
             num_scalar_prefetch=1,
             grid=(blocks,),
             in_specs=[whole(side), tile, whole(key_table), whole(value_table)],
-            out_specs=[tile, tile],
+            out_specs=[tile] * 3,
             scratch_shapes=pair,
         ),
         compiler_params=params,
@@ -326,7 +325,7 @@
         grid_spec=pltpu.PrefetchScalarGridSpec(
             num_scalar_prefetch=1,
             grid=(blocks,),
-            in_specs=[whole(side), tile, tile, tile] + [pl.BlockSpec(memory_space=pl.ANY)] * len(arrived),
+            in_specs=[whole(side), tile, tile, tile, tile] + [pl.BlockSpec(memory_space=pl.ANY)] * len(arrived),
             out_specs=tile,
             scratch_shapes=[
                 pltpu.VMEM((2, 2 * heads * len(arrived), block_len, head_dim), jnp.bfloat16),
@@ -336,7 +335,7 @@
         ),
         compiler_params=params,
         cost_estimate=cost,
-    )(plan, side, flat, partial_sum, stat, *arrived)
+    )(plan, side, flat, *partials, *arrived)
     return out.reshape(tokens_dev, query_heads, head_dim)
 
 

time: 146 us -> 98 us (0.67)
  the two profiles are of different devices: /device:TPU:26 before, /device:TPU:8 now
where the time goes in v3:
time: 98 us; the launch traced here: 96.6 us
  Pallas kernels  90.2 us (92%)
  starting transfers between devices  5.3 us (5%)
    pallas_call x1, Pallas kernels, on_device(): pl.pallas_call(functools.partial(local_kernel, heads, picks), out_shape=[...  43.9 us
    pallas_call x1, Pallas kernels, on_device(): pl.pallas_call(functools.partial(remote_kernel, heads, picks, blocks), ou...  35 us
    pallas_call x1, Pallas kernels, prepare(): pl.pallas_call(functools.partial(prepare_kernel, shards, query_heads), ou...  11.3 us
    ppermute x3, starting transfers between devices, on_device(): lax.ppermute(block, 'ctx', [(i, i + d) for i in range(shards - d)])  5.3 us
  transfers between devices with their start and end apart: 3, of which 0 were waited for; matrix products, arithmetic and copies ran while one was open for 0% of the time, Pallas kernels for 45%

profile of v3, /device:TPU:8, one launch (start us, length us, event | category | flops | bytes accessed | tf_op | source)
XLA Modules:
  0.0 96.6 jit_solution(8606289730116314074)
XLA Ops:
  0.0 0.0 copy-start
  0.0 0.7 copy-done
  0.7 11.3 %shard_map.46 = (s32[32,24]{1,0:T(8,128)S(1)}, bf16[2,24,128,128]{3,2,1,0:T(8,128)(2,1)S(1)}, bf16[2,24,128,128]{3,2,1,0:T(8,128)(2,1)S(1)}, bf16[2,4,128,128]{3...) custom-call(s32[4,8,24]{2,1,0:T(8,128)S(1)} %bitcast.5, ...), custom_call_target="tpu_custom_call" | custom-call | tf_op jit(solution)/shard_map/pallas_call | solution.py:146
  12.0 2.9 %collective-permute-start = (bf16[2,4,128,128]{3,2,1,0:T(8,128)(2,1)S(1)}, bf16[2,4,128,128]{3,2,1,0:T(8,128)(2,1)S(1)}, u32[]{:S(2)}, u32[]{:S(2)}) collective-permute-start(bf16[2,4,128,128]{3,2,1,0:T(8,128)(2,1)S(1)} %get-tuple-element.20), channel_id=1, source_target_pairs={{0,4},{4,8},{8,12},{1,5},{5,9},{9,13},{2,6},{6,10},{10,14},{3,7},{... | collective-permute-start | bytes 786440 | tf_op jit(solution)/shard_map/ppermute | solution.py:293
  14.9 1.8 %collective-permute-start.1 = (bf16[2,4,128,128]{3,2,1,0:T(8,128)(2,1)S(1)}, bf16[2,4,128,128]{3,2,1,0:T(8,128)(2,1)S(1)}, u32[]{:S(2)}, u32[]{:S(2)}) collective-permute-start(bf16[2,4,128,128]{3,2,1,0:T(8,128)(2,1)S(1)} %get-tuple-element.21), channel_id=1, source_target_pairs={{0,8},{4,12},{1,9},{5,13},{2,10},{6,14},{3,11},{7,15},{16,24},{20,... | collective-permute-start | bytes 786440 | tf_op jit(solution)/shard_map/ppermute | solution.py:293
  16.6 0.7 collective-permute-start.2
  17.4 0.1 broadcast_in_dim.2.side_ref
  17.5 43.9 %shard_map.47 = (f32[24576,128]{1,0:T(8,128)}, f32[24576,128]{1,0:T(8,128)}, f32[24576,128]{1,0:T(8,128)}) custom-call(s32[32,24]{1,0:T(8,128)S(1)} %get-tuple-element.14.plan_ref, bf16[2,256,128]{2,1,0:T(8,128)(2,1)S(1)} %broadcast_in_dim.2.side_ref, bf16[24576,128]{1,0:T(8,128)(2,1)} %bitcast.6, bf16[2,24,128,128]{3,2,1,0:T(8,128)(2,1)S(1)} %get-tuple-element.15.k_ref, ...), custom_call_target="tpu_custom_call" | custom-call | flops 12884901888 | bytes 37748736 | tf_op jit(solution)/shard_map/pallas_call | solution.py:309
  61.4 0.0 collective-permute-done.refs_0_
  61.4 0.0 collective-permute-done.1.refs_1_
  61.4 0.0 collective-permute-done.2.refs_2_
  61.4 35.0 %shard_map.48 = bf16[24576,128]{1,0:T(8,128)(2,1)} custom-call(s32[32,24]{1,0:T(8,128)S(1)} %get-tuple-element.14.plan_ref, bf16[2,256,128]{2,1,0:T(8,128)(2,1)S(1)} %broadcast_in_dim.2.side_ref, bf16[24576,128]{1,0:T(8,128)(2,1)} %bitcast.7, f32[24576,128]{1,0:T(8,128)} %get-tuple-element.17.sum_ref, f32[24576,128]{1,0:T(8,128)} %get-tuple-element.18.top_ref, ...), custom_call_target="tpu_custom_call" | custom-call | flops 12884901888 | bytes 37748736 | tf_op jit(solution)/shard_map/pallas_call | solution.py:322
  (2 shorter events, 0.0 us)
Async XLA Ops:
  0.0 0.7 copy-start
  12.0 49.4 %collective-permute-start = (bf16[2,4,128,128]{3,2,1,0:T(8,128)(2,1)S(1)}, bf16[2,4,128,128]{3,2,1,0:T(8,128)(2,1)S(1)}, u32[]{:S(2)}, u32[]{:S(2)}) collective-permute-start(bf16[2,4,128,128]{3,2,1,0:T(8,128)(2,1)S(1)} %get-tuple-element.20), channel_id=1, source_target_pairs={{0,4},{4,8},{8,12},{1,5},{5,9},{9,13},{2,6},{6,10},{10,14},{3,7},{... | collective-permute-start | bytes 786440 | tf_op jit(solution)/shard_map/ppermute | solution.py:293
  14.9 46.5 %collective-permute-start.1 = (bf16[2,4,128,128]{3,2,1,0:T(8,128)(2,1)S(1)}, bf16[2,4,128,128]{3,2,1,0:T(8,128)(2,1)S(1)}, u32[]{:S(2)}, u32[]{:S(2)}) collective-permute-start(bf16[2,4,128,128]{3,2,1,0:T(8,128)(2,1)S(1)} %get-tuple-element.21), channel_id=1, source_target_pairs={{0,8},{4,12},{1,9},{5,13},{2,10},{6,14},{3,11},{7,15},{16,24},{20,... | collective-permute-start | bytes 786440 | tf_op jit(solution)/shard_map/ppermute | solution.py:293
  16.6 44.8 %collective-permute-start.2 = (bf16[2,4,128,128]{3,2,1,0:T(8,128)(2,1)S(1)}, bf16[2,4,128,128]{3,2,1,0:T(8,128)(2,1)S(1)}, u32[]{:S(2)}, u32[]{:S(2)}) collective-permute-start(bf16[2,4,128,128]{3,2,1,0:T(8,128)(2,1)S(1)} %get-tuple-element.22), channel_id=1, source_target_pairs={{0,12},{1,13},{2,14},{3,15},{16,28},{17,29},{18,30},{19,31}} | collective-permute-start | bytes 786440 | tf_op jit(solution)/shard_map/ppermute | solution.py:293
